TPU v7x, 256 devices: a whole 4x4x8 slice. The times are simulated.
256 devices in a mesh: qrow: 16 (over x_hi, y, core), dbcol: 16 (over z, x_lo).
Axes of the slice: x: 4 (x_hi: 2, x_lo: 2; x = x_hi * 2 + x_lo), y: 4, z: 8, core: 2. Of those that a mesh axis runs over, the one named last changes fastest.
Arguments:
- query_desc: bfloat16 [8192, 1024], P('qrow', 'dbcol'), may hold values from -0.1875 to 0.1875
- base_desc: bfloat16 [4096, 1024], P('dbcol', 'qrow'), may hold values from -6 to 6
- slopes: int32 [5], replicated, may hold values from -3 to 3, as said below
Outputs:
- seq_score: bfloat16 [8192, 4096], P('qrow', 'dbcol')
- best_score: float32 [8192], P('qrow')
Inputs may be any that keep to these rules, and one draw needn't show every extreme that they name: `slopes`: 5 distinct values that always include -3 and 3.
All inputs are finite; a program needn't handle non-finite values.
Results may differ from a plain program's by a relative error of at most 0.0041.
Values may be sent and summed in bfloat16 or wider, within the bound.
No kernel may reach another device: no remote copies, remote signals or barrier semaphores. Data moves between devices by JAX's collectives and lax.ppermute only.
A program may use at most 64 MiB of HBM per device.

v0:
```python
import math

import jax
import jax.numpy as jnp
from jax import lax
from jax.experimental import pallas as pl
from jax.experimental.pallas import tpu as pltpu
from jax.sharding import PartitionSpec as P


SEQ = 20
PART = 5
SIDE = 64
PAD = 8
TAIL = 128
LANES = 128


def score_kernel(
    slopes, q_ref, tail_ref, own_ref, other_ref, out_ref, top_ref,
    similar, sums, squares, copies, part, part_late, half, half_late, best,
):
    rows, cols = out_ref.shape
    width = own_ref.shape[-1]
    features = own_ref.shape[1]
    depth = own_ref.shape[0] * features
    blocks = rows // LANES
    every = range(blocks + 1)
    parity = lax.rem(lax.axis_index("qrow"), 2)
    first_col = lax.axis_index("dbcol") * cols
    total_cols = lax.axis_size("dbcol") * cols

    def rows_at(start):
        return pl.ds(pl.multiple_of(start, 8), 8)

    def tiles(start, count, unroll, body):
        def step(index, carry):
            body(start + index * 8)
            return carry

        lax.fori_loop(0, count, step, 0, unroll=unroll)

    own = own_ref[...].reshape(depth, width)
    other = other_ref[...].reshape(depth, width)
    for ref, low, count, block in ((q_ref, 0, rows, 0), (tail_ref, 0, TAIL, blocks)):
        total = None
        for which, piece in ((parity, own), (1 - parity, other)):
            right = ref[:, which, :features, low : low + count].reshape(depth, count)
            product = lax.dot_general(
                piece, right, (((0,), (0,)), ((), ())), preferred_element_type=jnp.float32
            )
            total = product if total is None else total + product
        for c in range(count // LANES):
            similar[block + c, PAD : PAD + width, :] = total[:, c * LANES : (c + 1) * LANES]

    def five(r):
        for c in every:
            x = [similar[c, pl.ds(r + d, 8), :] for d in range(5)]
            sums[c, rows_at(r), :] = (x[0] + x[1]) + (x[2] + x[3]) + x[4]
            x = [v * v for v in x]
            squares[c, rows_at(r), :] = (x[0] + x[1]) + (x[2] + x[3]) + x[4]

    tiles(0, (width + PAD) // 8, 49, five)

    lane = lax.broadcasted_iota(jnp.int32, (8, LANES), 1)
    sublane = lax.broadcasted_iota(jnp.int32, (8, LANES), 0)

    def rolled(values, by):
        turned = [pltpu.roll(v, by, axis=1) for v in values]
        return [jnp.where(lane < by, turned[c - 1], turned[c]) for c in range(len(values))]

    def normalise(r):
        col = sublane + (first_col + r - PAD - SIDE)
        low = jnp.maximum(col - 5, 0)
        high = jnp.minimum(col + 5, total_cols)
        inverse = 1.0 / jnp.maximum(high - low, 1).astype(jnp.float32)
        keep = jnp.where((col >= 0) & (col < total_cols), 1.0, 0.0)
        values = []
        for c in every:
            mean = (sums[c, pl.ds(r - 5, 8), :] + sums[c, rows_at(r), :]) * inverse
            square = (squares[c, pl.ds(r - 5, 8), :] + squares[c, rows_at(r), :]) * inverse
            var = square - mean * mean
            value = (similar[c, rows_at(r), :] - mean) * lax.rsqrt(jnp.maximum(var, 0.25)) * keep
            values.append(value.astype(jnp.bfloat16).astype(jnp.float32))
        for k in range(PART):
            for c, v in enumerate(rolled(values, k) if k else values):
                copies[k, c, rows_at(r), :] = v

    tiles(PAD, width // 8, 24, normalise)

    first = PAD + SIDE

    def one_slope(at, carry):
        slope = slopes[at]
        down = slope > 0
        start_half = jnp.where(down, first - 32, first)
        start_part = jnp.where(down, first - 48, first)

        def add_part(r):
            values = []
            for c in every:
                x = [copies[k, c, pl.ds(r - slope * k, 8), :] for k in range(PART)]
                values.append((x[0] + x[1]) + (x[2] + x[3]) + x[4])
            for c, v in enumerate(values):
                part[c, rows_at(r), :] = v
            for c, v in enumerate(rolled(values, PART)):
                part_late[c, rows_at(r), :] = v

        def add_half(r):
            values = [
                part[c, rows_at(r), :] + part_late[c, pl.ds(r - slope * PART, 8), :] for c in every
            ]
            for c, v in enumerate(values[:-1]):
                half[c, rows_at(r), :] = v
            for c, v in enumerate(rolled(values, 2 * PART)[:-1]):
                half_late[c, rows_at(r), :] = v

        def finish(r):
            for c in range(blocks):
                total = half[c, rows_at(r), :] + half_late[c, pl.ds(r - slope * 2 * PART, 8), :]
                best[c, rows_at(r - first), :] = jnp.maximum(
                    best[c, rows_at(r - first), :], total
                )

        tiles(start_part, (cols + 48) // 8, 38, add_part)
        tiles(start_half, (cols + 32) // 8, 36, add_half)
        tiles(first, cols // 8, 32, finish)
        return carry

    best[...] = jnp.full(best.shape, -jnp.inf, jnp.float32)
    lax.fori_loop(0, slopes.shape[0], one_slope, 0)

    scale = 1.0 / math.sqrt(SEQ)
    for c in range(blocks):
        scores = best[c] * scale
        out_ref[c * LANES : (c + 1) * LANES, :] = scores.T.astype(jnp.bfloat16)
        top_ref[:, c * LANES : (c + 1) * LANES] = jnp.max(scores, axis=0, keepdims=True)


def pack_kernel(query_ref, base_ref, out_ref):
    features, cols = base_ref.shape
    here = lax.axis_index("dbcol")
    base = base_ref[...].astype(jnp.float32)

    def packed(low):
        pieces = [base[at : at + 8, low : low + SIDE] for at in range(0, features, 8)]
        return jnp.concatenate(pieces, axis=1).astype(jnp.bfloat16)

    low, high = packed(0), packed(cols - SIDE)
    query = query_ref[...]
    for peer in range(out_ref.shape[0]):
        out_ref[peer, :features, :] = query
        out_ref[peer, features:, :] = jnp.where(peer > here, high, low)


def widen_kernel(all_ref, base_ref, out_ref, edges, sems):
    features, _ = base_ref.shape
    here = lax.axis_index("dbcol")
    last = lax.axis_size("dbcol") - 1
    copies = []
    for at, peer in enumerate((jnp.maximum(here - 1, 0), jnp.minimum(here + 1, last))):
        source = all_ref.at[peer, pl.ds(features, 8), :]
        copies.append(pltpu.make_async_copy(source, edges.at[at], sems.at[at]))
        copies[-1].start()
    for copy in copies:
        copy.wait()

    def unpacked(at, inside):
        edge = jnp.where(inside, edges[at].astype(jnp.float32), 0.0)
        pieces = [edge[:, low : low + SIDE] for low in range(0, edge.shape[1], SIDE)]
        return jnp.concatenate(pieces, axis=0)

    base = base_ref[...].astype(jnp.float32)
    wide = [unpacked(0, here > 0), base, unpacked(1, here < last)]
    wide = jnp.concatenate(wide, axis=1).astype(jnp.bfloat16)
    for peer in range(out_ref.shape[0]):
        out_ref[peer] = wide


def broadcast_to(x, peers):
    return jnp.broadcast_to(x[None], (peers,) + x.shape)


def whole(query_desc, base_desc, slopes):
    rows, cols = query_desc.shape[0], base_desc.shape[0]
    across, down = lax.axis_size("dbcol"), lax.axis_size("qrow")
    query = query_desc.T
    base = base_desc.T
    depth = query.shape[0]

    vmem = pl.BlockSpec(memory_space=pltpu.VMEM)
    blocks = pl.pallas_call(
        pack_kernel,
        out_shape=jax.ShapeDtypeStruct((across, depth + 8, rows), jnp.bfloat16),
        in_specs=[vmem, vmem],
        out_specs=vmem,
        name="pack",
    )(query, base)
    query_all = lax.all_to_all(blocks, "dbcol", 0, 0)
    tail = lax.ppermute(
        query_all[:, :depth, rows - TAIL :], "qrow", [(i, i + 1) for i in range(down - 1)]
    )
    wide = pl.pallas_call(
        widen_kernel,
        out_shape=jax.ShapeDtypeStruct((down // 2, depth, cols + 2 * SIDE), jnp.bfloat16),
        in_specs=[pl.BlockSpec(memory_space=pl.ANY), vmem],
        out_specs=vmem,
        scratch_shapes=[
            pltpu.VMEM((2, 8, rows), jnp.bfloat16),
            pltpu.SemaphoreType.DMA((2,)),
        ],
        name="widen",
    )(query_all, base)
    same_core = [[2 * k + core for k in range(down // 2)] for core in range(2)]
    own = lax.all_to_all(wide, "qrow", 0, 0, axis_index_groups=same_core)
    other = lax.ppermute(own, "qrow", [(i, i ^ 1) for i in range(down)])

    def tall(lead):
        return pltpu.VMEM(lead + (cols + 2 * SIDE + 2 * PAD, LANES), jnp.float32)

    scores, top = pl.pallas_call(
        score_kernel,
        out_shape=(
            jax.ShapeDtypeStruct((rows, cols), jnp.bfloat16),
            jax.ShapeDtypeStruct((1, rows), jnp.float32),
        ),
        in_specs=[pl.BlockSpec(memory_space=pltpu.SMEM), vmem, vmem, vmem, vmem],
        out_specs=(vmem, vmem),
        scratch_shapes=[
            tall((rows // LANES + 1,)),
            tall((rows // LANES + 1,)),
            tall((rows // LANES + 1,)),
            tall((PART, rows // LANES + 1)),
            tall((rows // LANES + 1,)),
            tall((rows // LANES + 1,)),
            tall((rows // LANES,)),
            tall((rows // LANES,)),
            pltpu.VMEM((rows // LANES, cols, LANES), jnp.float32),
        ],
        name="score",
    )(
        slopes,
        query_all.reshape(across // 2, 2, depth + 8, rows),
        tail.reshape(across // 2, 2, depth, TAIL),
        own,
        other,
    )
    tops = lax.all_to_all(broadcast_to(top, across), "dbcol", 0, 0)
    return scores, jnp.max(tops[:, 0], axis=0)


def solution(mesh):
    placed = (P("qrow", "dbcol"), P("dbcol", "qrow"), P())
    return jax.shard_map(
        whole,
        mesh=mesh,
        in_specs=placed,
        out_specs=(P("qrow", "dbcol"), P("qrow")),
        check_vma=False,
    )
```

profile of v0, /device:TPU:4, one launch (start us, length us, event | category | flops | bytes accessed | tf_op | source)
XLA Modules:
  0.0 95.1 jit_solution(9318093203618830911)
XLA Ops:
  0.6 2.0 %pack.1 = bf16[16,72,512]{2,1,0:T(8,128)(2,1)} custom-call(bf16[64,512]{1,0:T(8,128)(2,1)} %bitcast.9, bf16[64,256]{1,0:T(8,128)(2,1)} %bitcast.7), custom_call_target="tpu_custom_call" | custom-call | tf_op jit(solution)/shard_map/pack/pallas_call | solution.py:192
  2.6 41.4 %all_to_all.15.all_ref = bf16[16,72,512]{2,1,0:T(8,128)(2,1)} all-to-all(bf16[16,72,512]{2,1,0:T(8,128)(2,1)} %pack.1), channel_id=1, replica_groups=mesh['qrow'=16,'dbcol'=16] {'dbcol'}, dimensions={0} | all-to-all | bytes 2359296 | tf_op jit(solution)/shard_map/all_to_all | solution.py:199
  44.0 2.4 %widen.1 = bf16[8,64,384]{2,1,0:T(8,128)(2,1)} custom-call(bf16[16,72,512]{2,1,0:T(8,128)(2,1)} %all_to_all.15.all_ref, bf16[64,256]{1,0:T(8,128)(2,1)} %bitcast.8), custom_call_target="tpu_custom_call" | custom-call | tf_op jit(solution)/shard_map/widen/pallas_call | solution.py:203
  46.4 14.1 %all_to_all.16.own_ref = bf16[8,64,384]{2,1,0:T(8,128)(2,1)S(1)} all-to-all(bf16[8,64,384]{2,1,0:T(8,128)(2,1)} %widen.1), channel_id=1, replica_groups={{0,32,64,96,128,160,192,224},{16,48,80,112,144,176,208,240},{1,33,65,97..., dimensions={0} | all-to-all | bytes 786432 | tf_op jit(solution)/shard_map/all_to_all | solution.py:215
  60.5 0.0 copy-start
  60.5 0.0 collective-permute-start.1
  60.5 1.1 %slice.4 = bf16[16,64,128]{2,1,0:T(8,128)(2,1)S(1)} slice(bf16[16,72,512]{2,1,0:T(8,128)(2,1)} %all_to_all.15.all_ref), slice={[0:16], [0:64], [384:512]} | slice | bytes 524288 | tf_op jit(solution)/shard_map/slice | solution.py:201
  61.6 2.3 %collective-permute-start = (bf16[16,64,128]{2,1,0:T(8,128)(2,1)S(1)}, bf16[16,64,128]{2,1,0:T(8,128)(2,1)S(1)}, u32[]{:S(2)}, u32[]{:S(2)}) collective-permute-start(bf16[16,64,128]{2,1,0:T(8,128)(2,1)S(1)} %slice.4), channel_id=1, source_target_pairs={{0,16},{16,32},{32,48},{48,64},{64,80},{80,96},{96,112},{112,128},... | collective-permute-start | bytes 786440 | tf_op jit(solution)/shard_map/ppermute | solution.py:200
  63.9 9.0 %collective-permute-done = bf16[16,64,128]{2,1,0:T(8,128)(2,1)S(1)} collective-permute-done((bf16[16,64,128]{2,1,0:T(8,128)(2,1)S(1)}, bf16[16,64,128]{2,1,0:T(8,128)(2,1)S(1)}, u32[]{:S(2)}, u32[]{:S(2)}) %collective-permute-start) | collective-permute-done | bytes 262176 | tf_op jit(solution)/shard_map/ppermute | solution.py:200
  72.9 0.0 copy-start.2
  72.9 0.0 collective-permute-done.1.other_ref
  72.9 0.0 copy-start.1
  72.9 0.0 copy-done
  72.9 0.7 copy-done.2
  73.6 0.1 copy-done.1
  73.8 8.4 %score.1 = (bf16[512,256]{1,0:T(8,128)(2,1)}, f32[1,512]{1,0:T(1,128)}) custom-call(s32[5]{0:T(128)} %slopes.1, bf16[8,2,72,512]{3,2,1,0:T(8,128)(2,1)} %bitcast.5, bf16[8,2,64,128]{3,2,1,0:T(8,128)(2,1)} %bitcast.6, bf16[8,64,384]{2,1,0:T(8,128)(2,1)} %copy-done, bf16[8,64,384]{2,1,0:T(8,128)(2,1)} %copy-done.1), custom_call_target="tpu_custom_call" | custom-call | tf_op jit(solution)/shard_map/score/pallas_call | solution.py:221
  82.2 0.7 broadcast_in_dim.9
  82.9 11.6 %all_to_all.17 = f32[16,1,512]{2,1,0:T(1,128)S(1)} all-to-all(f32[16,1,512]{2,1,0:T(1,128)S(1)} %broadcast_in_dim.9), channel_id=1, replica_groups=mesh['qrow'=16,'dbcol'=16] {'dbcol'}, dimensions={0} | all-to-all | bytes 65536 | tf_op jit(solution)/shard_map/all_to_all | solution.py:248
  94.4 0.6 reduce_max.9
Async XLA Ops:
  60.5 12.4 %copy-start = (bf16[8,64,384]{2,1,0:T(8,128)(2,1)}, bf16[8,64,384]{2,1,0:T(8,128)(2,1)S(1)}, u32[]{:S(2)}) copy-start(bf16[8,64,384]{2,1,0:T(8,128)(2,1)S(1)} %all_to_all.16.own_ref) | copy-start | bytes 1179652
  60.5 12.4 %collective-permute-start.1 = (bf16[8,64,384]{2,1,0:T(8,128)(2,1)S(1)}, bf16[8,64,384]{2,1,0:T(8,128)(2,1)S(1)}, u32[]{:S(2)}, u32[]{:S(2)}) collective-permute-start(bf16[8,64,384]{2,1,0:T(8,128)(2,1)S(1)} %all_to_all.16.own_ref), channel_id=1, source_target_pairs={{0,16},{16,0},{32,48},{48,32},{64,80},{80,64},{96,112},{112,96},{1... | collective-permute-start | bytes 1179656 | tf_op jit(solution)/shard_map/ppermute | solution.py:216
  61.6 11.3 %collective-permute-start = (bf16[16,64,128]{2,1,0:T(8,128)(2,1)S(1)}, bf16[16,64,128]{2,1,0:T(8,128)(2,1)S(1)}, u32[]{:S(2)}, u32[]{:S(2)}) collective-permute-start(bf16[16,64,128]{2,1,0:T(8,128)(2,1)S(1)} %slice.4), channel_id=1, source_target_pairs={{0,16},{16,32},{32,48},{48,64},{64,80},{80,96},{96,112},{112,128},... | collective-permute-start | bytes 786440 | tf_op jit(solution)/shard_map/ppermute | solution.py:200
  72.9 0.7 copy-start.2
  72.9 0.8 copy-start.1
where the time goes:
time: 95.6 us; the launch traced here: 95.1 us
  blocking collectives  67 us (70%)
  Pallas kernels  12.8 us (13%)
  waiting for transfers between devices  9.03 us (9%)
  local copies, waits for them, and re-layouts  2.67 us (3%)
  starting transfers between devices  2.28 us (2%)
    all_to_all x1, blocking collectives, whole(): query_all = lax.all_to_all(blocks, 'dbcol', 0, 0)  41.4 us
    all_to_all x1, blocking collectives, whole(): own = lax.all_to_all(wide, 'qrow', 0, 0, axis_index_groups=same_core)  14.1 us
    all_to_all x1, blocking collectives, whole(): tops = lax.all_to_all(broadcast_to(top, across), 'dbcol', 0, 0)  11.6 us
    ppermute x1, waiting for transfers between devices, whole(): lax.ppermute(query_all[:, :depth, rows - TAIL:], 'qrow', [(i, i + 1) for...  9.02 us
    pallas_call x1, Pallas kernels, whole(): pl.pallas_call(score_kernel, out_shape=(jax.ShapeDtypeStruct((rows, cols)...  8.4 us
    pallas_call x1, Pallas kernels, whole(): pl.pallas_call(widen_kernel, out_shape=jax.ShapeDtypeStruct((down // 2, d...  2.41 us
    ppermute x1, starting transfers between devices, whole(): lax.ppermute(query_all[:, :depth, rows - TAIL:], 'qrow', [(i, i + 1) for...  2.27 us
    pallas_call x1, Pallas kernels, whole(): pl.pallas_call(pack_kernel, out_shape=jax.ShapeDtypeStruct((across, depth...  1.97 us
  transfers between devices with their start and end apart: 2, of which 1 were waited for; matrix products, arithmetic and copies ran while one was open for 1% of the time, Pallas kernels for 0%

commit v1 on v0

--- a/solution.py
+++ b/solution.py
@@ -86,7 +86,7 @@
             for c, v in enumerate(rolled(values, k) if k else values):
                 copies[k, c, rows_at(r), :] = v
 
-    tiles(PAD, width // 8, 24, normalise)
+    tiles(PAD, width // 8, 48, normalise)
 
     first = PAD + SIDE
 
@@ -134,12 +134,13 @@
     for c in range(blocks):
         scores = best[c] * scale
         out_ref[c * LANES : (c + 1) * LANES, :] = scores.T.astype(jnp.bfloat16)
-        top_ref[:, c * LANES : (c + 1) * LANES] = jnp.max(scores, axis=0, keepdims=True)
+        most = jnp.max(scores, axis=0, keepdims=True)
+        for peer in range(top_ref.shape[0]):
+            top_ref[peer, :, c * LANES : (c + 1) * LANES] = most
 
 
 def pack_kernel(query_ref, base_ref, out_ref):
     features, cols = base_ref.shape
-    here = lax.axis_index("dbcol")
     base = base_ref[...].astype(jnp.float32)
 
     def packed(low):
@@ -148,33 +149,29 @@
 
     low, high = packed(0), packed(cols - SIDE)
     query = query_ref[...]
-    for peer in range(out_ref.shape[0]):
-        out_ref[peer, :features, :] = query
-        out_ref[peer, features:, :] = jnp.where(peer > here, high, low)
-
-
-def widen_kernel(all_ref, base_ref, out_ref, edges, sems):
+    for at, edge in enumerate((low, high)):
+        out_ref[at, :features, :] = query
+        out_ref[at, features:, :] = edge
+
+
+def widen_kernel(all_ref, base_ref, out_ref):
     features, _ = base_ref.shape
     here = lax.axis_index("dbcol")
     last = lax.axis_size("dbcol") - 1
-    copies = []
-    for at, peer in enumerate((jnp.maximum(here - 1, 0), jnp.minimum(here + 1, last))):
-        source = all_ref.at[peer, pl.ds(features, 8), :]
-        copies.append(pltpu.make_async_copy(source, edges.at[at], sems.at[at]))
-        copies[-1].start()
-    for copy in copies:
-        copy.wait()
-
-    def unpacked(at, inside):
-        edge = jnp.where(inside, edges[at].astype(jnp.float32), 0.0)
+
+    def unpacked(peer, inside):
+        edge = all_ref[jnp.clip(peer, 0, last), features:, :].astype(jnp.float32)
+        edge = jnp.where(inside, edge, 0.0)
         pieces = [edge[:, low : low + SIDE] for low in range(0, edge.shape[1], SIDE)]
         return jnp.concatenate(pieces, axis=0)
 
     base = base_ref[...].astype(jnp.float32)
-    wide = [unpacked(0, here > 0), base, unpacked(1, here < last)]
-    wide = jnp.concatenate(wide, axis=1).astype(jnp.bfloat16)
-    for peer in range(out_ref.shape[0]):
-        out_ref[peer] = wide
+    wide = [unpacked(here - 1, here > 0), base, unpacked(here + 1, here < last)]
+    out_ref[...] = jnp.concatenate(wide, axis=1).astype(jnp.bfloat16)
+
+
+def kept(x):
+    return pltpu.with_memory_space_constraint(x, pltpu.VMEM)
 
 
 def broadcast_to(x, peers):
@@ -189,30 +186,28 @@
     depth = query.shape[0]
 
     vmem = pl.BlockSpec(memory_space=pltpu.VMEM)
-    blocks = pl.pallas_call(
+    pair = pl.pallas_call(
         pack_kernel,
-        out_shape=jax.ShapeDtypeStruct((across, depth + 8, rows), jnp.bfloat16),
+        out_shape=jax.ShapeDtypeStruct((2, depth + 8, rows), jnp.bfloat16),
         in_specs=[vmem, vmem],
         out_specs=vmem,
         name="pack",
     )(query, base)
+    ahead = (jnp.arange(across) > lax.axis_index("dbcol"))[:, None, None]
+    blocks = jnp.where(ahead, pair[1][None], pair[0][None])
     query_all = lax.all_to_all(blocks, "dbcol", 0, 0)
     tail = lax.ppermute(
         query_all[:, :depth, rows - TAIL :], "qrow", [(i, i + 1) for i in range(down - 1)]
     )
     wide = pl.pallas_call(
         widen_kernel,
-        out_shape=jax.ShapeDtypeStruct((down // 2, depth, cols + 2 * SIDE), jnp.bfloat16),
-        in_specs=[pl.BlockSpec(memory_space=pl.ANY), vmem],
+        out_shape=jax.ShapeDtypeStruct((depth, cols + 2 * SIDE), jnp.bfloat16),
+        in_specs=[vmem, vmem],
         out_specs=vmem,
-        scratch_shapes=[
-            pltpu.VMEM((2, 8, rows), jnp.bfloat16),
-            pltpu.SemaphoreType.DMA((2,)),
-        ],
         name="widen",
-    )(query_all, base)
+    )(kept(query_all), base)
     same_core = [[2 * k + core for k in range(down // 2)] for core in range(2)]
-    own = lax.all_to_all(wide, "qrow", 0, 0, axis_index_groups=same_core)
+    own = lax.all_to_all(broadcast_to(wide, down // 2), "qrow", 0, 0, axis_index_groups=same_core)
     other = lax.ppermute(own, "qrow", [(i, i ^ 1) for i in range(down)])
 
     def tall(lead):
@@ -222,7 +217,7 @@
         score_kernel,
         out_shape=(
             jax.ShapeDtypeStruct((rows, cols), jnp.bfloat16),
-            jax.ShapeDtypeStruct((1, rows), jnp.float32),
+            jax.ShapeDtypeStruct((across, 1, rows), jnp.float32),
         ),
         in_specs=[pl.BlockSpec(memory_space=pltpu.SMEM), vmem, vmem, vmem, vmem],
         out_specs=(vmem, vmem),
@@ -240,12 +235,12 @@
         name="score",
     )(
         slopes,
-        query_all.reshape(across // 2, 2, depth + 8, rows),
-        tail.reshape(across // 2, 2, depth, TAIL),
-        own,
-        other,
+        kept(query_all.reshape(across // 2, 2, depth + 8, rows)),
+        kept(tail.reshape(across // 2, 2, depth, TAIL)),
+        kept(own),
+        kept(other),
     )
-    tops = lax.all_to_all(broadcast_to(top, across), "dbcol", 0, 0)
+    tops = lax.all_to_all(top, "dbcol", 0, 0)
     return scores, jnp.max(tops[:, 0], axis=0)
 
 

time: 95.6 us -> 92.6 us (0.969)
  Pallas kernels: 12.8 us -> 10.4 us
    pallas_call x2, Pallas kernels: 4.38 us -> 3.11 us  [the longest x1 1.58 us: whole(): pl.pallas_call(pack_kernel, out_shape=jax.ShapeDtypeStruct((2, depth + 8,...]
    pallas_call x1, Pallas kernels: 8.4 us -> 7.3 us  [whole(): pl.pallas_call(score_kernel, out_shape=(jax.ShapeDtypeStruct((rows, cols)...]
    slice x1, local copies, waits for them, and re-layouts: 1.13 us -> 0.06 us  [whole(): query_all[:, :depth, rows - TAIL:]]
  transfers between devices with their start and end apart: 2 -> 2, of which waited for: 1 -> 1; matrix products, arithmetic and copies ran while one was open for 1% -> 0% of each run, Pallas kernels for 0% -> 0%
where the time goes in v1:
time: 92.6 us; the launch traced here: 92.1 us
  blocking collectives  67.1 us (72%)
  Pallas kernels  10.4 us (11%)
  waiting for transfers between devices  8.88 us (10%)
  starting transfers between devices  2.42 us (3%)
  local copies, waits for them, and re-layouts  1.82 us (2%)
    all_to_all x1, blocking collectives, whole(): query_all = lax.all_to_all(blocks, 'dbcol', 0, 0)  41.1 us
    all_to_all x1, blocking collectives, whole(): lax.all_to_all(broadcast_to(wide, down // 2), 'qrow', 0, 0, axis_index_gr...  13.9 us
    all_to_all x1, blocking collectives, whole(): tops = lax.all_to_all(top, 'dbcol', 0, 0)  12.2 us
    ppermute x1, waiting for transfers between devices, whole(): lax.ppermute(query_all[:, :depth, rows - TAIL:], 'qrow', [(i, i + 1) for...  8.88 us
    pallas_call x1, Pallas kernels, whole(): pl.pallas_call(score_kernel, out_shape=(jax.ShapeDtypeStruct((rows, cols)...  7.3 us
    ppermute x1, starting transfers between devices, whole(): lax.ppermute(query_all[:, :depth, rows - TAIL:], 'qrow', [(i, i + 1) for...  2.41 us
  transfers between devices with their start and end apart: 2, of which 1 were waited for; matrix products, arithmetic and copies ran while one was open for 0% of the time, Pallas kernels for 0%

profile of v1, /device:TPU:4, one launch (start us, length us, event | category | flops | bytes accessed | tf_op | source)
XLA Modules:
  0.0 92.1 jit_solution(7980404601547220381)
XLA Ops:
  0.6 1.6 %pack.1 = bf16[2,72,512]{2,1,0:T(8,128)(2,1)} custom-call(bf16[64,512]{1,0:T(8,128)(2,1)} %bitcast.12, bf16[64,256]{1,0:T(8,128)(2,1)} %bitcast.10), custom_call_target="tpu_custom_call" | custom-call | tf_op jit(solution)/shard_map/pack/pallas_call | solution.py:189
  2.2 0.9 %slice_bitcast_fusion.1 = (bf16[72,512]{1,0:T(8,128)(2,1)S(1)}, bf16[72,512]{1,0:T(8,128)(2,1)S(1)}) fusion(bf16[2,72,512]{2,1,0:T(8,128)(2,1)} %pack.1), kind=kLoop, calls=%fused_computation.2 | loop fusion | bytes 294912 | tf_op jit(solution)/shard_map/jit(_where)/broadcast_in_dim | solution.py:197
  3.2 0.1 broadcast_select_fusion
  3.3 41.1 %all_to_all.15.all_ref = bf16[16,72,512]{2,1,0:T(8,128)(2,1)S(1)} all-to-all(bf16[16,72,512]{2,1,0:T(8,128)(2,1)S(1)} %broadcast_select_fusion), channel_id=1, replica_groups=mesh['qrow'=16,'dbcol'=16] {'dbcol'}, dimensions={0} | all-to-all | bytes 2359296 | tf_op jit(solution)/shard_map/all_to_all | solution.py:198
  44.4 1.5 %widen.1 = bf16[64,384]{1,0:T(8,128)(2,1)} custom-call(bf16[16,72,512]{2,1,0:T(8,128)(2,1)S(1)} %all_to_all.15.all_ref, bf16[64,256]{1,0:T(8,128)(2,1)} %bitcast.11), custom_call_target="tpu_custom_call" | custom-call | tf_op jit(solution)/shard_map/widen/pallas_call | solution.py:202
  45.9 0.8 broadcast_in_dim.40
  46.8 13.9 %all_to_all.16.own_ref = bf16[8,64,384]{2,1,0:T(8,128)(2,1)S(1)} all-to-all(bf16[8,64,384]{2,1,0:T(8,128)(2,1)S(1)} %broadcast_in_dim.40), channel_id=1, replica_groups={{0,32,64,96,128,160,192,224},{16,48,80,112,144,176,208,240},{1,33,65,97..., dimensions={0} | all-to-all | bytes 786432 | tf_op jit(solution)/shard_map/all_to_all | solution.py:210
  60.6 0.0 collective-permute-start.1
  60.6 0.1 slice.14
  60.7 2.4 %collective-permute-start = (bf16[16,64,128]{2,1,0:T(8,128)(2,1)S(1)}, bf16[16,64,128]{2,1,0:T(8,128)(2,1)S(1)}, u32[]{:S(2)}, u32[]{:S(2)}) collective-permute-start(bf16[16,64,128]{2,1,0:T(8,128)(2,1)S(1)} %slice.14), channel_id=1, source_target_pairs={{0,16},{16,32},{32,48},{48,64},{64,80},{80,96},{96,112},{112,128},... | collective-permute-start | bytes 786440 | tf_op jit(solution)/shard_map/ppermute | solution.py:199
  63.1 8.9 %collective-permute-done = bf16[16,64,128]{2,1,0:T(8,128)(2,1)S(1)} collective-permute-done((bf16[16,64,128]{2,1,0:T(8,128)(2,1)S(1)}, bf16[16,64,128]{2,1,0:T(8,128)(2,1)S(1)}, u32[]{:S(2)}, u32[]{:S(2)}) %collective-permute-start) | collective-permute-done | bytes 262176 | tf_op jit(solution)/shard_map/ppermute | solution.py:199
  72.0 0.0 collective-permute-done.1.other_ref
  72.0 7.3 %score.1 = (bf16[512,256]{1,0:T(8,128)(2,1)}, f32[16,1,512]{2,1,0:T(1,128)}) custom-call(s32[5]{0:T(128)} %slopes.1, bf16[8,2,72,512]{3,2,1,0:T(8,128)(2,1)S(1)} %bitcast.8, bf16[8,2,64,128]{3,2,1,0:T(8,128)(2,1)S(1)} %bitcast.9, bf16[8,64,384]{2,1,0:T(8,128)(2,1)S(1)} %all_to_all.16.own_ref, bf16[8,64,384]{2,1,0:T(8,128)(2,1)S(1)} %collective-permute-done.1.other_ref), custom_call_target="tpu_custom_call" | custom-call | tf_op jit(solution)/shard_map/score/pallas_call | solution.py:216
  79.3 12.2 %all_to_all.17 = f32[16,1,512]{2,1,0:T(1,128)S(1)} all-to-all(f32[16,1,512]{2,1,0:T(1,128)} %get-tuple-element.5), channel_id=1, replica_groups=mesh['qrow'=16,'dbcol'=16] {'dbcol'}, dimensions={0} | all-to-all | bytes 65536 | tf_op jit(solution)/shard_map/all_to_all | solution.py:243
  91.5 0.6 reduce_max.9
  (1 shorter events, 0.0 us)
Async XLA Ops:
  60.6 11.4 %collective-permute-start.1 = (bf16[8,64,384]{2,1,0:T(8,128)(2,1)S(1)}, bf16[8,64,384]{2,1,0:T(8,128)(2,1)S(1)}, u32[]{:S(2)}, u32[]{:S(2)}) collective-permute-start(bf16[8,64,384]{2,1,0:T(8,128)(2,1)S(1)} %all_to_all.16.own_ref), channel_id=1, source_target_pairs={{0,16},{16,0},{32,48},{48,32},{64,80},{80,64},{96,112},{112,96},{1... | collective-permute-start | bytes 1179656 | tf_op jit(solution)/shard_map/ppermute | solution.py:211
  60.7 11.3 %collective-permute-start = (bf16[16,64,128]{2,1,0:T(8,128)(2,1)S(1)}, bf16[16,64,128]{2,1,0:T(8,128)(2,1)S(1)}, u32[]{:S(2)}, u32[]{:S(2)}) collective-permute-start(bf16[16,64,128]{2,1,0:T(8,128)(2,1)S(1)} %slice.14), channel_id=1, source_target_pairs={{0,16},{16,32},{32,48},{48,64},{64,80},{80,96},{96,112},{112,128},... | collective-permute-start | bytes 786440 | tf_op jit(solution)/shard_map/ppermute | solution.py:199
